TPU v7x, 32 devices: a whole 2x2x4 slice. The times are simulated.
32 devices in a mesh: cfg: 4 (over z), mode: 8 (over y, x, core).
Axes of the slice: x: 2, y: 2, z: 4, core: 2. Of those that a mesh axis runs over, the one named last changes fastest.
Arguments:
- coords: bfloat16 [10368, 2048], P('mode', 'cfg'), may hold values from -6 to 6
- curvature: float32 [10368], P('mode'), may hold values from 0.2 to 5
- weight: float32 [10368], P('mode'), may hold values from 0.3 to 3
- polar: bfloat16 [10368, 10368], P('mode'), may hold values from -0.078125 to 0.078125
- forces: bfloat16 [10368, 2048], P('mode', 'cfg'), may hold values from -6 to 6
Outputs:
- gradient: float32 [10368, 10368], P('cfg', 'mode')
All inputs are finite; a program needn't handle non-finite values.
Results may differ from a plain program's by a relative error of at most 0.019.
Values may be sent and summed in bfloat16 or wider, within the bound.
A program may use at most 192 MiB of HBM per device.

v0:
```python
import math
import jax
import jax.numpy as jnp
from jax import lax
from jax.sharding import PartitionSpec as P


def on_device(coords, curvature, weight, polar, forces):
    f32 = jnp.float32
    bf16 = jnp.bfloat16
    configs_dev = coords.shape[1]
    scaled = (coords.astype(f32) * curvature[:, None]).astype(bf16)
    weighted = (coords.astype(f32) * weight[:, None]).astype(bf16)
    contract = (((0,), (0,)), ((), ()))
    shares = lax.psum_scatter(
        lax.dot_general(polar, scaled, contract, preferred_element_type=f32).astype(jnp.bfloat16),
        "mode",
        scatter_dimension=0,
        tiled=True,
    ).astype(jnp.float32)
    resid_rows = (forces.astype(f32) + shares).astype(bf16)
    residual = lax.all_gather(resid_rows, "mode", axis=0, tiled=True)
    factor = 1.0 / math.sqrt(configs_dev * lax.axis_size("cfg"))
    across = (((1,), (1,)), ((), ()))
    return lax.psum_scatter(
        (lax.dot_general(residual, weighted, across, preferred_element_type=f32) * factor).astype(
            jnp.bfloat16
        ),
        "cfg",
        scatter_dimension=0,
        tiled=True,
    ).astype(jnp.float32)


def solution(mesh):
    placed = (P("mode", "cfg"), P("mode"), P("mode"), P("mode", None), P("mode", "cfg"))
    return jax.shard_map(
        on_device, mesh=mesh, in_specs=placed, out_specs=P("cfg", "mode"), check_vma=False
    )
```

profile of v0, /device:TPU:0, one launch (start us, length us, event | category | flops | bytes accessed | tf_op | source)
XLA Modules:
  0.0 746.0 jit_solution(12773726648723765596)
XLA Ops:
  6.5 0.0 reduce-scatter.5.cloned.1.call-start
  6.5 23.2 %fusion = bf16[10368,512]{1,0:T(8,128)(2,1)} fusion(bf16[1296,10368]{1,0:T(8,128)(2,1)} %param.8, bf16[1296,512]{1,0:T(8,128)(2,1)} %param.5, f32[1296]{0:T(1024)} %param.6), kind=kOutput, calls=%fused_computation.2 | convolution fusion | flops 13766713344 | bytes 38822976 | tf_op jit(solution)/shard_map/dot_general | solution.py:16
  29.7 0.0 copy-start
  29.7 0.0 reduce-scatter.5.cloned.1.call-update
  29.7 0.0 copy-start.1
  29.7 0.0 copy-start.2
  29.7 0.0 all-gather.2.cloned.1.call-start
  29.8 85.4 %reduce-scatter.5.cloned.1.call-done = bf16[1296,512]{1,0:T(8,128)(2,1)} async-done(((bf16[10368,512]{1,0:T(8,128)(2,1)}), bf16[1296,512]{1,0:T(8,128)(2,1)}) %reduce-scatter.5.cloned.1.call-update) | async-done | bytes 1327120 | tf_op jit(solution)/shard_map/reduce_scatter | solution.py:15
  115.2 0.0 copy-done
  115.2 2.7 add_convert_fusion
  117.9 0.0 all-gather.2.cloned.1.call-update
  118.0 0.2 reduce-scatter.7.cloned.1.call-start
  118.2 63.6 %all-gather.2.cloned.1.call-done = bf16[10368,512]{1,0:T(8,128)(2,1)} async-done(((bf16[1296,512]{1,0:T(8,128)(2,1)}), bf16[10368,512]{1,0:T(8,128)(2,1)}) %all-gather.2.cloned.1.call-update) | async-done | bytes 10616848 | tf_op jit(solution)/shard_map/all_gather | solution.py:22
  181.8 0.0 copy-done.1
  181.8 0.0 copy-done.2
  181.8 22.4 %multiply_convert_fusion = bf16[10368,1296]{0,1:T(8,128)(2,1)} fusion(bf16[10368,512]{1,0:T(8,128)(2,1)} %all-gather.2.cloned.1.call-done, bf16[1296,512]{1,0:T(8,128)(2,1)S(1)} %copy-done.1, f32[1296]{0:T(1024)S(1)} %copy-done.2), kind=kOutput, calls=%fused_computation | convolution fusion | flops 13788278784 | bytes 38822976 | tf_op jit(solution)/shard_map/dot_general | solution.py:26
  204.2 35.9 %copy.6 = bf16[10368,1296]{1,0:T(8,128)(2,1)} copy(bf16[10368,1296]{0,1:T(8,128)(2,1)} %multiply_convert_fusion) | data formatting | bytes 53747712
  240.1 0.0 reduce-scatter.7.cloned.1.call-update
  240.2 479.6 %reduce-scatter.7.cloned.1.call-done = bf16[2592,1296]{1,0:T(8,128)(2,1)} async-done(((bf16[10368,1296]{1,0:T(8,128)(2,1)}), bf16[2592,1296]{1,0:T(8,128)(2,1)}) %reduce-scatter.7.cloned.1.call-update) | async-done | bytes 6718480
  719.7 10.6 %copy.7 = bf16[2592,1296]{0,1:T(8,128)(2,1)} copy(bf16[2592,1296]{1,0:T(8,128)(2,1)} %reduce-scatter.7.cloned.1.call-done) | data formatting | bytes 13436928
  730.4 9.1 %convert_element_type.40 = f32[2592,1296]{0,1:T(8,128)} convert(bf16[2592,1296]{0,1:T(8,128)(2,1)} %copy.7) | non-fusion elementwise | flops 3359232 | bytes 20155392 | tf_op jit(solution)/shard_map/convert_element_type | solution.py:32
Async XLA Ops:
  6.5 108.7 %reduce-scatter.5.cloned.1.call-start = ((), (), s32[]{:S(2)}) async-start(), calls=%async_computation.2 | async-start | bytes 11943936 | tf_op jit(solution)/shard_map/reduce_scatter | solution.py:15
  29.7 85.5 %copy-start = (bf16[1296,512]{1,0:T(8,128)(2,1)S(1)}, bf16[1296,512]{1,0:T(8,128)(2,1)}, u32[]{:S(2)}) copy-start(bf16[1296,512]{1,0:T(8,128)(2,1)} %param.9) | copy-start | bytes 3981316
  29.7 152.1 %copy-start.1 = (bf16[1296,512]{1,0:T(8,128)(2,1)S(1)}, bf16[1296,512]{1,0:T(8,128)(2,1)}, u32[]{:S(2)}) copy-start(bf16[1296,512]{1,0:T(8,128)(2,1)} %param.5) | copy-start | bytes 3981316
  29.7 152.1 %copy-start.2 = (f32[1296]{0:T(1024)S(1)}, f32[1296]{0:T(1024)}, u32[]{:S(2)}) copy-start(f32[1296]{0:T(1024)} %param.7) | copy-start | bytes 15556
  29.7 152.0 %all-gather.2.cloned.1.call-start = ((), (), s32[]{:S(2)}) async-start(), calls=%async_computation.3 | async-start | bytes 11943936 | tf_op jit(solution)/shard_map/all_gather | solution.py:22
  118.0 601.7 %reduce-scatter.7.cloned.1.call-start = ((), (), s32[]{:S(2)}) async-start(), calls=%async_computation.4 | async-start | bytes 36495360
Sparse Core Ops, SparseCore 0:
  29.8 85.3 reduce-scatter.4
  118.1 63.6 all-gather.1
  240.3 479.3 reduce-scatter.6
where the time goes:
time: 747 us; the launch traced here: 746 us
  waiting for transfers between devices  629 us (84%)
  local copies, waits for them, and re-layouts  46.6 us (6%)
  matrix products  45.6 us (6%)
  between operations  13.1 us (2%)
  other arithmetic  11.8 us (2%)
    unnamed x4, waiting for transfers between devices  480 us
    reduce_scatter x1, waiting for transfers between devices, on_device(): lax.psum_scatter(lax.dot_general(polar, scaled, contract, preferred_eleme...  85.4 us
    all_gather x1, waiting for transfers between devices, on_device(): residual = lax.all_gather(resid_rows, 'mode', axis=0, tiled=True)  63.6 us
    unnamed x8, local copies, waits for them, and re-layouts  46.6 us
    dot_general x1, matrix products, on_device(): lax.dot_general(polar, scaled, contract, preferred_element_type=f32)  23.2 us
    dot_general x1, matrix products, on_device(): lax.dot_general(residual, weighted, across, preferred_element_type=f32)  22.4 us
  transfers between devices with their start and end apart: 3, of which 3 were waited for; matrix products, arithmetic and copies ran while one was open for 0% of the time, Pallas kernels for 0%

commit v1 on v0

--- a/solution.py
+++ b/solution.py
@@ -3,6 +3,34 @@
 import jax.numpy as jnp
 from jax import lax
 from jax.sharding import PartitionSpec as P
+from jax.lax import axis_index, axis_size, ppermute
+
+
+def trace_the_series_all(u_in, dimension_no):
+    u_in = jnp.moveaxis(u_in, 0, dimension_no)
+    odd = u_in.shape
+    v1 = u_in.reshape(
+        *odd[:dimension_no], odd[dimension_no] * odd[dimension_no + 1], *odd[dimension_no + 2 :]
+    )
+    return v1
+
+
+def assign_fields(chunk, bus_axis):
+    p_count = axis_size(bus_axis)
+    shaped = chunk[None]
+    for ii in range(p_count.bit_length() - 1):
+        after = 1 << ii
+        line_up = []
+        hop_no = 0
+        while hop_no < p_count:
+            line_up.append((hop_no, hop_no ^ after))
+            hop_no += 1
+        h_now = ppermute(shaped, axis_name=bus_axis, perm=line_up)
+        before = jnp.stack([shaped, h_now], axis=0)
+        raw_out = axis_index(bus_axis)
+        heard = raw_out >> ii & 1
+        shaped = jnp.where(heard == 0, before, before[::-1]).reshape(-1, *chunk.shape)
+    return shaped
 
 
 def on_device(coords, curvature, weight, polar, forces):
@@ -19,7 +47,8 @@
         tiled=True,
     ).astype(jnp.float32)
     resid_rows = (forces.astype(f32) + shares).astype(bf16)
-    residual = lax.all_gather(resid_rows, "mode", axis=0, tiled=True)
+    earlier = assign_fields(resid_rows, "mode")
+    residual = trace_the_series_all(earlier, 0)
     factor = 1.0 / math.sqrt(configs_dev * lax.axis_size("cfg"))
     across = (((1,), (1,)), ((), ()))
     return lax.psum_scatter(

time: 747 us -> 918 us (1.23)
  waiting for transfers between devices: 629 us -> 739 us
  local copies, waits for them, and re-layouts: 46.6 us -> 83.6 us
  other arithmetic: 11.8 us -> 30.5 us
    ppermute x0 -> x3, waiting for transfers between devices: none -> 176 us  [assign_fields(): h_now = ppermute(shaped, axis_name=bus_axis, perm=line_up)]
    reduce_scatter x1 -> x0, waiting for transfers between devices: 85.4 us -> none  [on_device(): lax.psum_scatter(lax.dot_general(polar, scaled, contract, preferred_eleme...]
    unnamed x4, waiting for transfers between devices: 480 us -> 563 us
    all_gather x1 -> x0, waiting for transfers between devices: 63.6 us -> none  [on_device(): residual = lax.all_gather(resid_rows, 'mode', axis=0, tiled=True)]
    unnamed x8 -> x15, local copies, waits for them, and re-layouts: 46.6 us -> 64.8 us
    another operation x0 -> x5, other arithmetic: none -> 12.4 us  [assign_fields(): before = jnp.stack([shaped, h_now], axis=0)]
  transfers between devices with their start and end apart: 3 -> 5, of which waited for: 3 -> 5; matrix products, arithmetic and copies ran while one was open for 0% -> 0% of each run, Pallas kernels for 0% -> 0%
where the time goes in v1:
time: 918 us; the launch traced here: 916 us
  waiting for transfers between devices  739 us (81%)
  local copies, waits for them, and re-layouts  83.6 us (9%)
  matrix products  46.3 us (5%)
  other arithmetic  30.5 us (3%)
  between operations  13.5 us (1%)
    unnamed x4, waiting for transfers between devices  563 us
    ppermute x3, waiting for transfers between devices, assign_fields(): h_now = ppermute(shaped, axis_name=bus_axis, perm=line_up)  176 us
    unnamed x15, local copies, waits for them, and re-layouts  64.8 us
    dot_general x1, matrix products, on_device(): lax.dot_general(polar, scaled, contract, preferred_element_type=f32)  23.9 us
    dot_general x1, matrix products, on_device(): lax.dot_general(residual, weighted, across, preferred_element_type=f32)  22.4 us
  transfers between devices with their start and end apart: 5, of which 5 were waited for; matrix products, arithmetic and copies ran while one was open for 0% of the time, Pallas kernels for 0%

profile of v1, /device:TPU:0, one launch (start us, length us, event | category | flops | bytes accessed | tf_op | source)
XLA Modules:
  0.0 916.1 jit_solution(14061544266081663681)
XLA Ops:
  6.5 23.9 %fusion = bf16[10368,512]{0,1:T(8,128)(2,1)} fusion(bf16[1296,10368]{1,0:T(8,128)(2,1)} %param.8, bf16[1296,512]{1,0:T(8,128)(2,1)} %param.5, f32[1296]{0:T(1024)} %param.6), kind=kOutput, calls=%fused_computation.3 | convolution fusion | flops 13766713344 | bytes 38822976 | tf_op jit(solution)/shard_map/dot_general | solution.py:44
  30.4 14.5 %copy.17 = bf16[10368,512]{1,0:T(8,128)(2,1)} copy(bf16[10368,512]{0,1:T(8,128)(2,1)} %fusion) | data formatting | bytes 21233664
  44.9 0.0 reduce-scatter.7.cloned.1.call-update
  45.0 0.2 reduce-scatter.9.cloned.1.call-start
  45.2 1.1 copy-done.2
  46.2 0.8 copy.10
  47.1 83.4 %reduce-scatter.7.cloned.1.call-done = bf16[1296,512]{1,0:T(8,128)(2,1)} async-done(((bf16[10368,512]{1,0:T(8,128)(2,1)}), bf16[1296,512]{1,0:T(8,128)(2,1)}) %reduce-scatter.7.cloned.1.call-update) | async-done | bytes 1327120
  130.4 1.8 copy.18
  132.2 1.9 fusion.10
  134.2 1.7 copy.11
  135.9 0.1 collective-permute-start
  136.0 3.2 collective-permute-done
  139.2 1.8 copy.12
  141.0 0.3 pad_maximum_fusion.2
  141.3 2.2 fusion.4
  143.5 2.7 copy.13
  146.2 1.5 collective-permute-start.1
  147.6 58.5 %collective-permute-done.1 = bf16[2,1296,512]{2,1,0:T(8,128)(2,1)} collective-permute-done((bf16[2,1296,512]{2,1,0:T(8,128)(2,1)}, bf16[2,1296,512]{2,1,0:T(8,128)(2,1)}, u32[]{:S(2)}, u32[]{:S(2)}) %collective-permute-start.1) | collective-permute-done | bytes 2654240 | tf_op jit(solution)/shard_map/ppermute | solution.py:28
  206.1 4.5 copy.14
  210.6 2.4 pad_maximum_fusion.1
  213.0 3.7 reverse_select_fusion.1
  216.8 8.0 copy.15
  224.8 1.5 collective-permute-start.2
  226.3 114.5 %collective-permute-done.2 = bf16[4,1296,512]{2,1,0:T(8,128)(2,1)} collective-permute-done((bf16[4,1296,512]{2,1,0:T(8,128)(2,1)}, bf16[4,1296,512]{2,1,0:T(8,128)(2,1)}, u32[]{:S(2)}, u32[]{:S(2)}) %collective-permute-start.2) | collective-permute-done | bytes 5308448 | tf_op jit(solution)/shard_map/ppermute | solution.py:28
  340.8 5.5 pad_maximum_fusion
  346.3 5.3 reverse_select_fusion
  351.6 22.4 %multiply_convert_fusion = bf16[10368,1296]{0,1:T(8,128)(2,1)} fusion(bf16[10368,512]{1,0:T(8,128)(2,1)} %bitcast.23, bf16[1296,512]{1,0:T(8,128)(2,1)S(1)} %copy-done.3, f32[1296]{0:T(1024)S(1)} %copy-done.4), kind=kOutput, calls=%fused_computation | convolution fusion | flops 13788278784 | bytes 38822976 | tf_op jit(solution)/shard_map/dot_general | solution.py:55
  374.0 35.9 %copy.19 = bf16[10368,1296]{1,0:T(8,128)(2,1)} copy(bf16[10368,1296]{0,1:T(8,128)(2,1)} %multiply_convert_fusion) | data formatting | bytes 53747712
  410.0 0.0 reduce-scatter.9.cloned.1.call-update
  410.0 479.5 %reduce-scatter.9.cloned.1.call-done = bf16[2592,1296]{1,0:T(8,128)(2,1)} async-done(((bf16[10368,1296]{1,0:T(8,128)(2,1)}), bf16[2592,1296]{1,0:T(8,128)(2,1)}) %reduce-scatter.9.cloned.1.call-update) | async-done | bytes 6718480
  889.5 10.7 %copy.20 = bf16[2592,1296]{0,1:T(8,128)(2,1)} copy(bf16[2592,1296]{1,0:T(8,128)(2,1)} %reduce-scatter.9.cloned.1.call-done) | data formatting | bytes 13436928
  900.2 9.1 convert_element_type.40
  (10 shorter events, 0.0 us)
Async XLA Ops:
  6.5 123.9 %reduce-scatter.7.cloned.1.call-start = ((), (), s32[]{:S(2)}) async-start(), calls=%async_computation.2 | async-start | bytes 11943936
  44.9 1.3 copy-start.2
  45.0 844.5 %reduce-scatter.9.cloned.1.call-start = ((), (), s32[]{:S(2)}) async-start(), calls=%async_computation.3 | async-start | bytes 36495360
  134.2 6.8 copy-start.1
  135.9 3.3 collective-permute-start
  146.2 64.4 %copy-start = (bf16[1,2,1296,512]{2,3,1,0:T(8,128)(2,1)S(1)}, bf16[1,2,1296,512]{2,3,1,0:T(8,128)(2,1)}, u32[]{:S(2)}) copy-start(bf16[1,2,1296,512]{2,3,1,0:T(8,128)(2,1)} %get-tuple-element.5) | copy-start | bytes 7962628
  146.2 59.9 %collective-permute-start.1 = (bf16[2,1296,512]{2,1,0:T(8,128)(2,1)}, bf16[2,1296,512]{2,1,0:T(8,128)(2,1)}, u32[]{:S(2)}, u32[]{:S(2)}) collective-permute-start(bf16[2,1296,512]{2,1,0:T(8,128)(2,1)} %copy.13), channel_id=1, source_target_pairs={{0,2},{1,3},{2,0},{3,1},{4,6},{5,7},{6,4},{7,5},{8,10},{9,11},{10,... | collective-permute-start | bytes 7962632 | tf_op jit(solution)/shard_map/ppermute | solution.py:28
  224.8 115.9 %collective-permute-start.2 = (bf16[4,1296,512]{2,1,0:T(8,128)(2,1)}, bf16[4,1296,512]{2,1,0:T(8,128)(2,1)}, u32[]{:S(2)}, u32[]{:S(2)}) collective-permute-start(bf16[4,1296,512]{2,1,0:T(8,128)(2,1)} %bitcast.20), channel_id=1, source_target_pairs={{0,4},{1,5},{2,6},{3,7},{4,0},{5,1},{6,2},{7,3},{8,12},{9,13},{10,... | collective-permute-start | bytes 15925256 | tf_op jit(solution)/shard_map/ppermute | solution.py:28
  346.2 5.4 copy-start.3
  346.3 5.3 copy-start.4
Sparse Core Ops, SparseCore 0:
  45.1 85.3 reduce-scatter.6
  410.1 479.3 reduce-scatter.8
